TPU v7x, 128 devices: a whole 4x4x4 slice. The times are simulated.
128 devices in a mesh: tm: 32 (over y, x, core), gz: 4 (over z).
Axes of the slice: x: 4, y: 4, z: 4, core: 2. Of those that a mesh axis runs over, the one named last changes fastest.
Arguments:
- state_rhs: float32 [128, 128, 2048], P('tm', 'gz'), may hold values from -6 to 6
- adjoint_rhs: float32 [128, 128, 2048], P('tm', 'gz'), may hold values from -6 to 6
- diffusivity: float32 [128, 2048], P('gz'), may hold values from 0.02 to 2
- velocity: float32 [3, 128, 2048], P(None, 'gz'), may hold values from -4 to 4
Outputs:
- state_out: float32 [128, 128, 2048], P('tm', 'gz')
- adjoint_out: float32 [128, 128, 2048], P('tm', 'gz')
All inputs are finite; a program needn't handle non-finite values.
Results may differ from a plain program's by a relative error of at most 0.0003.
Values sent between devices are 32-bit elements; how exact they have to be, the bound alone decides.
A program may use at most 128 MiB of HBM per device.

v0:
```python
import math

import jax
import jax.numpy as jnp
from jax import lax
from jax.sharding import PartitionSpec as P

NY = 64


alpha_wrap = 0.1
beta_couple = 0.5
gamma_couple = 0.5


def padded(cells, sides, width):
    for axis, dim in sides:
        count = lax.axis_size(axis)
        ends = count - 1
        head = lax.slice_in_dim(cells, 0, width, axis=dim)
        tail = lax.slice_in_dim(cells, cells.shape[dim] - width, cells.shape[dim], axis=dim)
        cells = jnp.concatenate(
            [
                lax.ppermute(tail, axis, [(i, (i + 1) % count) for i in range(ends)]),
                cells,
                lax.ppermute(head, axis, [((i + 1) % count, i) for i in range(ends)]),
            ],
            axis=dim,
        )
    return cells


def swapped(value, axis, bit):
    mask = 2**bit
    pairs = [(source, source ^ mask) for source in range(lax.axis_size(axis))]
    return lax.ppermute(value, axis, pairs)


def ahead_flat(field, stride):
    pad_shape = field.shape[:-1] + (stride,)
    return jnp.concatenate([field[..., stride:], jnp.zeros(pad_shape, field.dtype)], axis=-1)


def behind_flat(field, stride):
    pad_shape = field.shape[:-1] + (stride,)
    return jnp.concatenate([jnp.zeros(pad_shape, field.dtype), field[..., :-stride]], axis=-1)


def neighbour_pairs(field, field_pad, width_y):
    column = jnp.arange(field.shape[-1], dtype=jnp.int32) % width_y
    nothing = jnp.zeros((), field.dtype)
    y_ahead = jnp.where(column == width_y - 1, nothing, ahead_flat(field, 1))
    y_behind = jnp.where(column == 0, nothing, behind_flat(field, 1))
    return [
        (field_pad[..., 2:, :], field_pad[..., :-2, :]),
        (ahead_flat(field, width_y), behind_flat(field, width_y)),
        (y_ahead, y_behind),
    ]


def face_weights(kappa, kappa_pad, width_y):
    pairs = neighbour_pairs(kappa, kappa_pad, width_y)
    weights = []
    diagonal = jnp.zeros_like(kappa)
    for ahead, behind in pairs:
        face_ahead = jnp.where(ahead > 0.0, 0.5 * (kappa + ahead), kappa)
        face_behind = jnp.where(behind > 0.0, 0.5 * (kappa + behind), kappa)
        weights.append((face_ahead, face_behind))
        diagonal = diagonal + face_ahead + face_behind
    return (weights, diagonal)


def coupling(field, field_pad, weights, velocity, width_y):
    sign = jnp.array([1.0, -1.0, 1.0, -1.0], field.dtype).reshape((4,) + (1,) * (field.ndim - 1))
    pairs = neighbour_pairs(field, field_pad, width_y)
    speeds = [velocity[2], velocity[0], velocity[1]]
    total = jnp.zeros_like(field)
    for index in range(3):
        ahead, behind = pairs[index]
        face_ahead, face_behind = weights[index]
        total = (
            total
            + face_ahead * ahead
            + face_behind * behind
            - sign * (0.5 * speeds[index]) * (ahead - behind)
        )
    return total


def apply_split(stacked, lam_real, lam_real_other, lam_imag, diagonal):
    shifted = lam_real + diagonal
    shifted_other = lam_real_other + diagonal
    determinant = shifted * shifted + lam_imag * lam_imag + beta_couple * gamma_couple
    determinant_other = (
        shifted_other * shifted_other + lam_imag * lam_imag + beta_couple * gamma_couple
    )
    state_real, adjoint_real, state_imag, adjoint_imag = (
        stacked[0],
        stacked[1],
        stacked[2],
        stacked[3],
    )
    out_state_real = (
        shifted * state_real + lam_imag * state_imag + beta_couple * adjoint_real
    ) / determinant
    out_state_imag = (
        shifted_other * state_imag - lam_imag * state_real + beta_couple * adjoint_imag
    ) / determinant_other
    out_adjoint_real = (
        shifted * adjoint_real - lam_imag * adjoint_imag - gamma_couple * state_real
    ) / determinant
    out_adjoint_imag = (
        shifted_other * adjoint_imag + lam_imag * adjoint_real - gamma_couple * state_imag
    ) / determinant_other
    return jnp.stack([out_state_real, out_adjoint_real, out_state_imag, out_adjoint_imag])


def mix_rows(matrix, data):
    return jnp.einsum("ab,sbm->sam", matrix, data, precision=lax.Precision.HIGHEST)


def body(state_rhs, adjoint_rhs, diffusivity, velocity):
    steps_local, depth, cells = state_rhs.shape
    ranks = lax.axis_size("tm")
    rank = lax.axis_index("tm")
    total = steps_local * ranks
    two_pi = 2.0 * math.pi
    ratio = alpha_wrap ** (1.0 / total)
    kappa_pad = padded(diffusivity, (("gz", 0),), 1)
    weights, diagonal = face_weights(diffusivity, kappa_pad, NY)
    fields = jnp.stack([state_rhs, adjoint_rhs])
    local_steps = jnp.arange(steps_local, dtype=jnp.int32)
    bits = ranks.bit_length() - 1
    times_here = rank * steps_local + local_steps
    damping = jnp.power(jnp.float32(alpha_wrap), times_here.astype(jnp.float32) / total)
    scaled = fields * damping[None, :, None, None]
    top = bits - 1
    partner = swapped(scaled, "tm", top)
    high = rank >> top & 1 == 1
    position = (rank & (1 << top) - 1).astype(jnp.float32)
    cosine = jnp.cos(math.pi * position / (1 << top))
    sine = jnp.sin(math.pi * position / (1 << top))
    spread = partner - scaled
    real_part = jnp.where(high, spread * cosine, scaled + partner)
    imag_part = jnp.where(high, -spread * sine, jnp.zeros_like(spread))
    data = jnp.concatenate([real_part, imag_part])
    for level in range(1, bits):
        bit = bits - 1 - level
        half = 1 << bit
        partner = swapped(data, "tm", bit)
        high = rank >> bit & 1 == 1
        position = (rank & half - 1).astype(jnp.float32)
        cosine = jnp.cos(math.pi * position / half)
        sine = jnp.sin(math.pi * position / half)
        spread = partner - data
        turned = jnp.concatenate(
            [spread[:2] * cosine + spread[2:] * sine, spread[2:] * cosine - spread[:2] * sine]
        )
        data = jnp.where(high, turned, data + partner)
    reversed_rank = jnp.zeros((), jnp.int32)
    for bit in range(bits):
        reversed_rank = reversed_rank + ((rank >> bit & 1) << bits - 1 - bit)
    frequency = reversed_rank + ranks * local_steps
    phase = (frequency[:, None] * local_steps[None, :] % total).astype(jnp.float32) * (
        two_pi / total
    )
    grid_real = jnp.cos(phase)
    grid_imag = -jnp.sin(phase)
    flat = data.reshape(4, steps_local, depth * cells)
    out_real = mix_rows(grid_real, flat[:2]) - mix_rows(grid_imag, flat[2:])
    out_imag = mix_rows(grid_real, flat[2:]) + mix_rows(grid_imag, flat[:2])
    blocks = jnp.concatenate([out_real, out_imag]).reshape(4, steps_local, depth, cells)
    angle = (frequency % total).astype(jnp.float32) * (two_pi / total)
    lam_real = (1.0 - ratio * jnp.cos(angle)).reshape(steps_local, 1, 1)
    lam_imag = (ratio * jnp.sin(angle)).reshape(steps_local, 1, 1)
    first = apply_split(blocks, lam_real, lam_real, lam_imag, diagonal)
    first_pad = padded(first, (("gz", 2),), 1)
    solved = apply_split(
        blocks + coupling(first, first_pad, weights, velocity, NY),
        lam_real,
        lam_real,
        lam_imag,
        diagonal,
    )
    phase = (local_steps[:, None] * frequency[None, :] % total).astype(jnp.float32) * (
        two_pi / total
    )
    grid_real = jnp.cos(phase)
    grid_imag = jnp.sin(phase)
    flat = solved.reshape(4, steps_local, depth * cells)
    back_real = mix_rows(grid_real, flat[:2]) - mix_rows(grid_imag, flat[2:])
    back_imag = mix_rows(grid_real, flat[2:]) + mix_rows(grid_imag, flat[:2])
    data = jnp.concatenate([back_real, back_imag]).reshape(4, steps_local, depth, cells)
    for bit in range(bits):
        half = 1 << bit
        partner = swapped(data, "tm", bit)
        high = rank >> bit & 1 == 1
        position = (rank & half - 1).astype(jnp.float32)
        cosine = jnp.cos(math.pi * position / half)
        sine = jnp.sin(math.pi * position / half)
        other = jnp.where(high, data, partner)
        base = jnp.where(high, partner, data)
        turned = jnp.concatenate(
            [other[:2] * cosine - other[2:] * sine, other[:2] * sine + other[2:] * cosine]
        )
        data = jnp.where(high, base - turned, base + turned)
    undo = jnp.power(jnp.float32(alpha_wrap), -times_here.astype(jnp.float32) / total) / total
    result = data[:2] * undo[None, :, None, None]
    return (result[0], result[1])


def solution(mesh):
    placed = (P("tm", "gz", None), P("tm", "gz", None), P("gz", None), P(None, "gz", None))
    return jax.shard_map(
        body,
        mesh=mesh,
        in_specs=placed,
        out_specs=(P("tm", "gz", None), P("tm", "gz", None)),
        check_vma=False,
    )
```

profile of v0, /device:TPU:1, one launch (start us, length us, event | category | flops | bytes accessed | tf_op | source)
XLA Modules:
  0.0 890.8 jit_solution(3531315405878219138)
XLA Ops:
  2.6 3.8 collective-permute-start.2
  6.6 45.1 %collective-permute-done.2 = f32[2,4,32,2048]{3,2,1,0:T(8,128)} collective-permute-done((f32[2,4,32,2048]{3,2,1,0:T(8,128)S(1)}, f32[2,4,32,2048]{3,2,1,0:T(8,128)}, u32[]{:S(2)}, u32[]{:S(2)}) %collective-permute-start.2) | collective-permute-done | bytes 2097184 | tf_op jit(solution)/shard_map/ppermute | solution.py:36
  51.6 2.5 add_select_fusion.4
  54.1 2.6 pad_maximum_fusion.8
  58.2 89.5 %collective-permute-done.3 = f32[4,4,32,2048]{3,2,1,0:T(8,128)} collective-permute-done((f32[4,4,32,2048]{3,2,1,0:T(8,128)}, f32[4,4,32,2048]{3,2,1,0:T(8,128)}, u32[]{:S(2)}, u32[]{:S(2)}) %collective-permute-start.3) | collective-permute-done | bytes 4194336 | tf_op jit(solution)/shard_map/ppermute | solution.py:36
  147.7 3.6 fusion.108
  153.0 5.5 maximum_select_fusion
  158.5 2.7 collective-permute-start.4
  161.3 88.8 %collective-permute-done.4 = f32[4,4,32,2048]{3,2,1,0:T(8,128)} collective-permute-done((f32[4,4,32,2048]{3,2,1,0:T(8,128)}, f32[4,4,32,2048]{3,2,1,0:T(8,128)}, u32[]{:S(2)}, u32[]{:S(2)}) %collective-permute-start.4) | collective-permute-done | bytes 4194336 | tf_op jit(solution)/shard_map/ppermute | solution.py:36
  250.1 4.2 sub.154
  254.9 6.8 maximum_select_fusion.1
  263.0 88.0 %collective-permute-done.5 = f32[4,4,32,2048]{3,2,1,0:T(8,128)} collective-permute-done((f32[4,4,32,2048]{3,2,1,0:T(8,128)}, f32[4,4,32,2048]{3,2,1,0:T(8,128)}, u32[]{:S(2)}, u32[]{:S(2)}) %collective-permute-start.5) | collective-permute-done | bytes 4194336 | tf_op jit(solution)/shard_map/ppermute | solution.py:36
  351.0 4.2 sub.156
  355.8 6.8 maximum_select_fusion.2
  362.6 4.0 collective-permute-start.6
  366.7 3.4 collective-permute-start.1
  376.2 4.2 sub.158
  380.9 4.8 maximum_select_fusion.3
  385.7 2.3 fusion.113
  387.9 2.7 slice.217
  390.6 3.7 slice.219
  394.3 4.0 fusion.55
  398.3 4.0 fusion.57
  402.3 4.2 fusion.2
  406.5 4.6 fusion.3
  411.3 2.9 pad_maximum_fusion.9
  414.4 2.8 fusion.6
  419.2 4.9 fusion.112
  424.0 3.5 collective-permute-start.8
  428.8 4.8 fusion.111
  433.6 6.2 reshape.290
  439.9 12.3 %subtract_add_fusion = f32[4,4,32,2048]{3,2,1,0:T(8,128)S(1)} fusion(f32[4,4,32,2048]{3,2,1,0:T(8,128)} %reshape.290, f32[4,4,32,2047]{3,2,1,0:T(8,128)} %get-tuple-element.28, f32[4,4,32,2047]{3,2,1,0:T(8,128)} %get-tuple-element.27, f32[4,4,32,1984]{3,2,1,0:T(8,128)} %get-tuple-element.26, f32[4,4,32,1984]{3,2,1,0:T(8,128)} %get-tuple-element.25, ...), kind=kLoop, calls=%fused_computation.41 | loop fusion | flops 32505856 | bytes 34078720 | tf_op jit(solution)/shard_map/add | solution.py:179
  455.8 2.7 slice.240
  458.5 4.9 fusion.51
  464.9 3.7 slice.239
  468.5 5.5 fusion.53
  474.0 4.3 fusion
  478.3 4.1 fusion.1
  482.4 2.9 pad_maximum_fusion.11
  485.4 6.1 reshape.291
  493.2 7.0 collective-permute-done.9
  500.2 3.0 broadcast_select_fusion
  508.5 89.7 %collective-permute-done.10 = f32[4,4,32,2048]{3,2,1,0:T(8,128)S(1)} collective-permute-done((f32[4,4,32,2048]{3,2,1,0:T(8,128)S(1)}, f32[4,4,32,2048]{3,2,1,0:T(8,128)S(1)}, u32[]{:S(2)}, u32[]{:S(2)}) %collective-permute-start.10) | collective-permute-done | bytes 4194336 | tf_op jit(solution)/shard_map/ppermute | solution.py:36
  602.0 3.1 collective-permute-start.11
  605.1 90.9 %collective-permute-done.11 = f32[4,4,32,2048]{3,2,1,0:T(8,128)S(1)} collective-permute-done((f32[4,4,32,2048]{3,2,1,0:T(8,128)S(1)}, f32[4,4,32,2048]{3,2,1,0:T(8,128)S(1)}, u32[]{:S(2)}, u32[]{:S(2)}) %collective-permute-start.11) | collective-permute-done | bytes 4194336 | tf_op jit(solution)/shard_map/ppermute | solution.py:36
  700.6 90.4 %collective-permute-done.12 = f32[4,4,32,2048]{3,2,1,0:T(8,128)S(1)} collective-permute-done((f32[4,4,32,2048]{3,2,1,0:T(8,128)S(1)}, f32[4,4,32,2048]{3,2,1,0:T(8,128)S(1)}, u32[]{:S(2)}, u32[]{:S(2)}) %collective-permute-start.12) | collective-permute-done | bytes 4194336 | tf_op jit(solution)/shard_map/ppermute | solution.py:36
  794.2 3.0 collective-permute-start.13
  797.2 89.5 %collective-permute-done.13 = f32[4,4,32,2048]{3,2,1,0:T(8,128)S(1)} collective-permute-done((f32[4,4,32,2048]{3,2,1,0:T(8,128)S(1)}, f32[4,4,32,2048]{3,2,1,0:T(8,128)S(1)}, u32[]{:S(2)}, u32[]{:S(2)}) %collective-permute-start.13) | collective-permute-done | bytes 4194336 | tf_op jit(solution)/shard_map/ppermute | solution.py:36
  (83 shorter events, 44.3 us)
Async XLA Ops:
  0.6 51.0 %copy-start.8 = (f32[4,32,2048]{2,1,0:T(8,128)S(1)}, f32[4,32,2048]{2,1,0:T(8,128)}, u32[]{:S(2)}) copy-start(f32[4,32,2048]{2,1,0:T(8,128)} %param.6) | copy-start | bytes 3145732
  2.6 49.0 %collective-permute-start.2 = (f32[2,4,32,2048]{3,2,1,0:T(8,128)S(1)}, f32[2,4,32,2048]{3,2,1,0:T(8,128)}, u32[]{:S(2)}, u32[]{:S(2)}) collective-permute-start(f32[2,4,32,2048]{3,2,1,0:T(8,128)S(1)} %maximum_multiply_fusion), channel_id=1, source_target_pairs={{0,64},{4,68},{8,72},{12,76},{16,80},{20,84},{24,88},{28,92},{32,9... | collective-permute-start | bytes 6291464 | tf_op jit(solution)/shard_map/ppermute | solution.py:36
  54.1 2.7 copy-start.1
  56.8 91.0 %collective-permute-start.3 = (f32[4,4,32,2048]{3,2,1,0:T(8,128)}, f32[4,4,32,2048]{3,2,1,0:T(8,128)}, u32[]{:S(2)}, u32[]{:S(2)}) collective-permute-start(f32[4,4,32,2048]{3,2,1,0:T(8,128)} %pad_maximum_fusion.8), channel_id=1, source_target_pairs={{0,32},{4,36},{8,40},{12,44},{16,48},{20,52},{24,56},{28,60},{32,0... | collective-permute-start | bytes 12582920 | tf_op jit(solution)/shard_map/ppermute | solution.py:36
  151.4 1.6 copy-start.2
  158.5 91.6 %collective-permute-start.4 = (f32[4,4,32,2048]{3,2,1,0:T(8,128)}, f32[4,4,32,2048]{3,2,1,0:T(8,128)}, u32[]{:S(2)}, u32[]{:S(2)}) collective-permute-start(f32[4,4,32,2048]{3,2,1,0:T(8,128)} %maximum_select_fusion), channel_id=1, source_target_pairs={{0,16},{4,20},{8,24},{12,28},{16,0},{20,4},{24,8},{28,12},{32,48},... | collective-permute-start | bytes 12582920 | tf_op jit(solution)/shard_map/ppermute | solution.py:36
  261.7 89.3 %collective-permute-start.5 = (f32[4,4,32,2048]{3,2,1,0:T(8,128)}, f32[4,4,32,2048]{3,2,1,0:T(8,128)}, u32[]{:S(2)}, u32[]{:S(2)}) collective-permute-start(f32[4,4,32,2048]{3,2,1,0:T(8,128)} %maximum_select_fusion.1), channel_id=1, source_target_pairs={{0,8},{4,12},{8,0},{12,4},{16,24},{20,28},{24,16},{28,20},{32,40},... | collective-permute-start | bytes 12582920 | tf_op jit(solution)/shard_map/ppermute | solution.py:36
  355.8 10.9 %copy-start.7 = (f32[32,2048]{1,0:T(8,128)S(1)}, f32[32,2048]{1,0:T(8,128)}, u32[]{:S(2)}) copy-start(f32[32,2048]{1,0:T(8,128)} %param.7) | copy-start | bytes 786436
  362.6 9.4 %copy-start.10 = (f32[3,32,2048]{2,1,0:T(8,128)S(1)}, f32[3,32,2048]{2,1,0:T(8,128)}, u32[]{:S(2)}) copy-start(f32[3,32,2048]{2,1,0:T(8,128)} %param.8) | copy-start | bytes 2359300
  362.6 9.5 %copy-start.15 = (f32[4]{0:T(128)S(1)}, f32[4]{0:T(128)}, u32[]{:S(2)}) copy-start(f32[4]{0:T(128)} %constant.115.clone) | copy-start | bytes 52
  362.6 13.6 %collective-permute-start.6 = (f32[4,4,32,2048]{3,2,1,0:T(8,128)}, f32[4,4,32,2048]{3,2,1,0:T(8,128)}, u32[]{:S(2)}, u32[]{:S(2)}) collective-permute-start(f32[4,4,32,2048]{3,2,1,0:T(8,128)} %maximum_select_fusion.2), channel_id=1, source_target_pairs={{0,4},{4,0},{8,12},{12,8},{16,20},{20,16},{24,28},{28,24},{32,36},... | collective-permute-start | bytes 12582920 | tf_op jit(solution)/shard_map/ppermute | solution.py:36
  366.7 7.3 collective-permute-start.1
  370.1 4.6 collective-permute-start
  371.7 42.6 %copy-start.11 = (f32[4]{0:T(128)}, f32[4]{0:T(128)S(1)}, u32[]{:S(2)}) copy-start(f32[4]{0:T(128)S(1)} %get-tuple-element.64) | copy-start | bytes 52
  374.0 40.4 %copy-start.13 = (f32[4]{0:T(128)}, f32[4]{0:T(128)S(1)}, u32[]{:S(2)}) copy-start(f32[4]{0:T(128)S(1)} %fusion.107) | copy-start | bytes 52
  394.3 4.0 copy-start.3
  417.2 1.0 copy-start.5
  424.0 15.8 %collective-permute-start.8 = (f32[4,4,1,2048]{3,2,1,0:T(1,128)}, f32[4,4,1,2048]{3,2,1,0:T(1,128)S(1)}, u32[]{:S(2)}, u32[]{:S(2)}) collective-permute-start(f32[4,4,1,2048]{3,2,1,0:T(1,128)} %get-tuple-element.24), channel_id=1, source_target_pairs={{0,1},{1,2},{2,3},{4,5},{5,6},{6,7},{8,9},{9,10},{10,11},{12,13},{... | collective-permute-start | bytes 393224 | tf_op jit(solution)/shard_map/ppermute | solution.py:24
  427.5 12.3 %collective-permute-start.7 = (f32[4,4,1,2048]{3,2,1,0:T(1,128)}, f32[4,4,1,2048]{3,2,1,0:T(1,128)}, u32[]{:S(2)}, u32[]{:S(2)}) collective-permute-start(f32[4,4,1,2048]{3,2,1,0:T(1,128)} %get-tuple-element.23), channel_id=1, source_target_pairs={{1,0},{2,1},{3,2},{5,4},{6,5},{7,6},{9,8},{10,9},{11,10},{13,12},{... | collective-permute-start | bytes 393224 | tf_op jit(solution)/shard_map/ppermute | solution.py:26
  439.8 12.3 %copy-start.12 = (f32[4]{0:T(128)S(1)}, f32[4]{0:T(128)}, u32[]{:S(2)}) copy-start(f32[4]{0:T(128)} %copy-done.11) | copy-start | bytes 52
  439.8 12.3 %copy-start.14 = (f32[4]{0:T(128)S(1)}, f32[4]{0:T(128)}, u32[]{:S(2)}) copy-start(f32[4]{0:T(128)} %copy-done.13) | copy-start | bytes 52
  458.5 4.9 copy-start.9
  468.5 5.5 copy-start.4
  468.5 5.5 copy-start.6
  491.5 8.7 collective-permute-start.9
  503.2 2.2 copy-start
  507.2 91.0 %collective-permute-start.10 = (f32[4,4,32,2048]{3,2,1,0:T(8,128)S(1)}, f32[4,4,32,2048]{3,2,1,0:T(8,128)S(1)}, u32[]{:S(2)}, u32[]{:S(2)}) collective-permute-start(f32[4,4,32,2048]{3,2,1,0:T(8,128)S(1)} %add_select_fusion.3), channel_id=1, source_target_pairs={{0,8},{4,12},{8,0},{12,4},{16,24},{20,28},{24,16},{28,20},{32,40},... | collective-permute-start | bytes 12582920 | tf_op jit(solution)/shard_map/ppermute | solution.py:36
  602.0 94.0 %collective-permute-start.11 = (f32[4,4,32,2048]{3,2,1,0:T(8,128)S(1)}, f32[4,4,32,2048]{3,2,1,0:T(8,128)S(1)}, u32[]{:S(2)}, u32[]{:S(2)}) collective-permute-start(f32[4,4,32,2048]{3,2,1,0:T(8,128)S(1)} %add_select_fusion.2), channel_id=1, source_target_pairs={{0,16},{4,20},{8,24},{12,28},{16,0},{20,4},{24,8},{28,12},{32,48},... | collective-permute-start | bytes 12582920 | tf_op jit(solution)/shard_map/ppermute | solution.py:36
  699.2 91.8 %collective-permute-start.12 = (f32[4,4,32,2048]{3,2,1,0:T(8,128)S(1)}, f32[4,4,32,2048]{3,2,1,0:T(8,128)S(1)}, u32[]{:S(2)}, u32[]{:S(2)}) collective-permute-start(f32[4,4,32,2048]{3,2,1,0:T(8,128)S(1)} %add_select_fusion.1), channel_id=1, source_target_pairs={{0,32},{4,36},{8,40},{12,44},{16,48},{20,52},{24,56},{28,60},{32,0... | collective-permute-start | bytes 12582920 | tf_op jit(solution)/shard_map/ppermute | solution.py:36
  794.2 92.5 %collective-permute-start.13 = (f32[4,4,32,2048]{3,2,1,0:T(8,128)S(1)}, f32[4,4,32,2048]{3,2,1,0:T(8,128)S(1)}, u32[]{:S(2)}, u32[]{:S(2)}) collective-permute-start(f32[4,4,32,2048]{3,2,1,0:T(8,128)S(1)} %add_select_fusion), channel_id=1, source_target_pairs={{0,64},{4,68},{8,72},{12,76},{16,80},{20,84},{24,88},{28,92},{32,9... | collective-permute-start | bytes 12582920 | tf_op jit(solution)/shard_map/ppermute | solution.py:36
where the time goes:
time: 901 us; the launch traced here: 891 us
  waiting for transfers between devices  680 us (75%)
  other arithmetic  98.3 us (11%)
  local copies, waits for them, and re-layouts  42 us (5%)
  matrix products  35.5 us (4%)
  starting transfers between devices  33 us (4%)
    ppermute x10, waiting for transfers between devices, swapped(): return lax.ppermute(value, axis, pairs)  679 us
    dot_general x8, matrix products, mix_rows(): jnp.einsum('ab,sbm->sam', matrix, data, precision=lax.Precision.HIGHEST)  35.5 us
    select_n x4, other arithmetic, body(): data = jnp.where(high, turned, data + partner)  23.9 us
    ppermute x10, starting transfers between devices, swapped(): return lax.ppermute(value, axis, pairs)  23.3 us
  transfers between devices with their start and end apart: 14, of which 10 were waited for; matrix products, arithmetic and copies ran while one was open for 2% of the time, Pallas kernels for 0%

commit v1 on v0

v1 whole, which is shorter than its diff:
```python
import functools

import jax
import jax.numpy as jnp
from jax import lax
from jax.experimental import pallas as pl
from jax.experimental.pallas import tpu as pltpu
from jax.sharding import PartitionSpec as P

NY = 64
ALPHA = 0.1
HALF = 0.5
LANES = 128
ROWS = 32
PAD = 8
MESH = pl.DeviceIdType.MESH


def kernel(chips, row, slabs, f_hbm, g_hbm, k_hbm, v_hbm, s_hbm, p_hbm, fg, kp, vel, ck, cn, w, out,
           tot, rx, ct, gat, ret, carr, c2, lsem, osem, ksend, krecv, zsend, zrecv, xsend, xrecv):
    tm = lax.axis_index("tm")
    gz = lax.axis_index("gz")
    chip = tm // 2
    core = tm % 2
    steps = f_hbm.shape[0]
    total = steps * 2 * chips
    q = ALPHA ** (1.0 / total)
    q2 = q * q
    other = (2 * chip + 1 - core, gz)
    up = (tm, lax.rem(gz + 1, slabs))
    down = (tm, lax.rem(gz + slabs - 1, slabs))

    def peer(i):
        y = lax.rem(chip // row + i // row, chips // row)
        x = lax.rem(lax.rem(chip, row) + lax.rem(i, row), row)
        return y * row + x

    def device(c):
        return (2 * c + core, gz)

    barrier = pltpu.get_barrier_semaphore()
    for d in (other, up, down):
        pl.semaphore_signal(barrier, inc=1, device_id=d, device_id_type=MESH)

    def greet(i, _):
        pl.semaphore_signal(barrier, inc=1, device_id=device(peer(i)), device_id_type=MESH)

    lax.fori_loop(1, chips, greet, None)

    def loads(n, j):
        lanes = pl.ds(pl.multiple_of(j * LANES, LANES), LANES)
        source, target = (
            (k_hbm.at[:, lanes], kp.at[j, pl.ds(PAD, ROWS), :]),
            (f_hbm.at[:, :, lanes], fg.at[j, pl.ds(0, steps)]),
            (g_hbm.at[:, :, lanes], fg.at[j, pl.ds(steps, steps)]),
            (v_hbm.at[:, :, lanes], vel.at[j]),
        )[n]
        return pltpu.make_async_copy(source, target, lsem.at[n, j])

    def load_some(which):
        def body(j, _):
            for n in which:
                loads(n, j).start()
        lax.fori_loop(0, chips, body, None)

    load_some((0,))
    load_some((1, 2))
    load_some((3,))

    def wait_kappa(j, _):
        loads(0, j).wait()

    lax.fori_loop(0, chips, wait_kappa, None)
    pl.semaphore_wait(barrier, chips - 1 + 3)

    def edge(direction):
        source, target, device_id = ((PAD + ROWS - 1, PAD - 1, up), (PAD, PAD + ROWS, down))[direction]
        return pltpu.make_async_remote_copy(
            src_ref=kp.at[:, pl.ds(source, 1), :], dst_ref=kp.at[:, pl.ds(target, 1), :],
            send_sem=ksend.at[direction], recv_sem=krecv.at[direction],
            device_id=device_id, device_id_type=MESH)

    edge(0).start()
    edge(1).start()
    edge(0).wait()
    edge(1).wait()

    lane = lax.broadcasted_iota(jnp.int32, (ROWS, LANES), 1)
    line = lax.broadcasted_iota(jnp.int32, (ROWS, LANES), 0)
    ycol = lax.rem(lane, NY)
    first_half = lane < NY

    def sides(ref, j, index):
        here = ref[(j,) + index + (pl.ds(PAD, ROWS),)]
        nxt = ref[(jnp.minimum(j + 1, chips - 1),) + index + (pl.ds(PAD, ROWS),)]
        prv = ref[(jnp.maximum(j - 1, 0),) + index + (pl.ds(PAD, ROWS),)]
        return here, [
            (ref[(j,) + index + (pl.ds(PAD + 1, ROWS),)], ref[(j,) + index + (pl.ds(PAD - 1, ROWS),)]),
            (pltpu.roll(jnp.where(first_half, nxt, here), NY, 1),
             pltpu.roll(jnp.where(first_half, here, prv), NY, 1)),
            (pltpu.roll(here, LANES - 1, 1), pltpu.roll(here, 1, 1)),
        ]

    def faces(j):
        here, pairs = sides(kp, j, ())
        inside = [
            (jnp.logical_or(line < ROWS - 1, gz < slabs - 1), jnp.logical_or(line > 0, gz > 0)),
            (jnp.logical_or(first_half, j < chips - 1), jnp.logical_or(jnp.logical_not(first_half), j > 0)),
            (ycol < NY - 1, ycol > 0),
        ]
        result = []
        for pair, ok in zip(pairs, inside):
            result.append([(jnp.where(m, 0.5 * (here + n), here), m) for n, m in zip(pair, ok)])
        return result

    def waves(j):
        return ck[j, 0], ck[j, 1], ck[j, 2], ck[j, 3]

    def totals(k, j, f, g, b1, b2, mf):
        mb = mf * q2
        fwd = b1 * f[0] + b2 * g[0]
        for n in range(1, steps):
            fwd = b1 * f[n] + b2 * g[n] + mf * fwd
        bwd = b1 * g[steps - 1] - b2 * f[steps - 1]
        for n in range(steps - 2, -1, -1):
            bwd = b1 * g[n] - b2 * f[n] + mb * bwd
        tot[k, 0, j] = fwd
        tot[k, 1, j] = bwd
        to_other(k, j).start()

    def to_other(k, j):
        return pltpu.make_async_remote_copy(
            src_ref=tot.at[k, 1 - core, j], dst_ref=rx.at[k, j],
            send_sem=xsend.at[k, 0, j], recv_sem=xrecv.at[k, 0, j],
            device_id=other, device_id_type=MESH)

    def to_owner(k, j):
        return pltpu.make_async_remote_copy(
            src_ref=ct.at[k, j], dst_ref=gat.at[k, chip],
            send_sem=xsend.at[k, 1, j], recv_sem=xrecv.at[k, 1, chip],
            device_id=device(j), device_id_type=MESH)

    def from_source(k, j):
        return pltpu.make_async_remote_copy(
            src_ref=ct.at[k, j], dst_ref=gat.at[k, j],
            send_sem=xsend.at[k, 1, j], recv_sem=xrecv.at[k, 1, j],
            device_id=device(j), device_id_type=MESH)

    def back(k, j):
        return pltpu.make_async_remote_copy(
            src_ref=ret.at[k, j], dst_ref=carr.at[k, core, chip],
            send_sem=xsend.at[k, 2, j], recv_sem=xrecv.at[k, 2, chip],
            device_id=device(j), device_id_type=MESH)

    def from_owner(k, j):
        return pltpu.make_async_remote_copy(
            src_ref=ret.at[k, j], dst_ref=carr.at[k, core, j],
            send_sem=xsend.at[k, 2, j], recv_sem=xrecv.at[k, 2, j],
            device_id=device(j), device_id_type=MESH)

    def to_other_back(k, j):
        return pltpu.make_async_remote_copy(
            src_ref=c2.at[k, j], dst_ref=carr.at[k, core, j],
            send_sem=xsend.at[k, 3, j], recv_sem=xrecv.at[k, 3, j],
            device_id=other, device_id_type=MESH)

    def from_other_back(k, j):
        return pltpu.make_async_remote_copy(
            src_ref=c2.at[k, j], dst_ref=carr.at[k, 1 - core, j],
            send_sem=xsend.at[k, 3, j], recv_sem=xrecv.at[k, 3, j],
            device_id=other, device_id_type=MESH)

    per_step = jnp.where(core == 0, 1.0, q2).astype(jnp.float32)
    wrap = jnp.where(core == 0, ALPHA, 1.0 / ALPHA).astype(jnp.float32)

    def own_power(j):
        m = ck[j, 2] * per_step
        for _ in range(steps.bit_length() - 1):
            m = m * m
        return m

    def gather(k):
        def send(i, _):
            j = peer(i)
            to_other(k, j).wait_recv()
            ct[k, j] = own_power(j) * tot[k, core, j] + rx[k, j]
            to_owner(k, j).start()

        lax.fori_loop(1, chips, send, None)
        to_other(k, chip).wait_recv()
        gat[k, chip] = own_power(chip) * tot[k, core, chip] + rx[k, chip]

    def scan(k):
        def arrive(i, _):
            from_source(k, peer(i)).wait_recv()

        lax.fori_loop(1, chips, arrive, None)
        m = own_power(chip)
        m = m * m

        def place(r):
            return jnp.where(core == 0, r, chips - 1 - r)

        def step(r, carry):
            return m * carry + gat[k, place(r)]

        whole = lax.fori_loop(0, chips, step, jnp.zeros((ROWS, LANES), jnp.float32))
        m_all = m
        for _ in range(chips.bit_length() - 1):
            m_all = m_all * m_all
        carry = wrap * whole / (1.0 - wrap * m_all)

        def spread(r, carry):
            ret[k, place(r)] = carry
            return m * carry + gat[k, place(r)]

        lax.fori_loop(0, chips, spread, carry)

        def send(i, _):
            back(k, peer(i)).start()

        lax.fori_loop(1, chips, send, None)
        carr[k, core, chip] = ret[k, chip]

        def relay(j):
            c2[k, j] = own_power(j) * carr[k, core, j] + tot[k, core, j]
            to_other_back(k, j).start()

        relay(chip)

        def receive(i, _):
            j = peer(i)
            from_owner(k, j).wait_recv()
            relay(j)

        lax.fori_loop(1, chips, receive, None)

    def solve(k, j, store):
        from_other_back(k, j).wait_recv()
        b1, b2, mf, kf = waves(j)
        mb, kb = mf * q2, kf * q2
        f = [fg[j, n] for n in range(steps)]
        g = [fg[j, steps + n] for n in range(steps)]
        fwd = [carr[k, 0, j]]
        for n in range(steps):
            fwd.append(b1 * f[n] + b2 * g[n] + mf * fwd[-1])
        bwd = [carr[k, 1, j]]
        for n in range(steps - 1, -1, -1):
            bwd.append(b1 * g[n] - b2 * f[n] + mb * bwd[-1])
        bwd = bwd[::-1]
        for n in range(steps):
            store(n, fwd[n + 1] + kb * bwd[n + 1])
            store(steps + n, bwd[n] - kf * fwd[n])

    def begin(i, _):
        j = peer(i)
        a = sum(face for pair in faces(j) for face, _ in pair)
        c = 1.0 + a
        cq = c * q
        m = (c * c + (q2 + HALF * HALF)) / cq
        less = ((c - q) * (c - q) + HALF * HALF) / cq
        rho = 2.0 / (m + jnp.sqrt(less * (m + 2.0)))
        beta = c - q * rho
        scale = rho / (cq * (1.0 - rho * rho))
        b1, b2, mf, kf = scale * beta, HALF * scale, rho * (1.0 / q), rho * (HALF / q) / beta
        ck[j, 0] = b1
        ck[j, 1] = b2
        ck[j, 2] = mf
        ck[j, 3] = kf
        loads(1, j).wait()
        loads(2, j).wait()
        totals(0, j, [fg[j, n] for n in range(steps)], [fg[j, steps + n] for n in range(steps)], b1, b2, mf)

    lax.fori_loop(1, chips + 1, lambda i, _: begin(lax.rem(i, chips), _), None)
    gather(0)

    def couple(j, _):
        loads(3, j).wait()
        sets = faces(j)
        for d, component in enumerate((2, 0, 1)):
            half = 0.5 * vel[j, component]
            (ahead, ok_ahead), (behind, ok_behind) = sets[d]
            for n, value, ok in ((0, ahead - half, ok_ahead), (1, behind + half, ok_behind),
                                 (6, ahead + half, ok_ahead), (7, behind - half, ok_behind)):
                cn[j, 2 * d + n] = jnp.where(ok, value, 0.0)

    lax.fori_loop(0, chips, couple, None)
    scan(0)

    def layer(direction, j):
        source, target, device_id = ((PAD + ROWS - 1, PAD - 1, up), (PAD, PAD + ROWS, down))[direction]
        return pltpu.make_async_remote_copy(
            src_ref=w.at[j, :, pl.ds(source, 1), :], dst_ref=w.at[j, :, pl.ds(target, 1), :],
            send_sem=zsend.at[direction, j], recv_sem=zrecv.at[direction, j],
            device_id=device_id, device_id_type=MESH)

    def first(i, _):
        j = peer(i)

        def store(n, value):
            w[j, n, pl.ds(PAD, ROWS)] = value

        solve(0, j, store)
        layer(0, j).start()
        layer(1, j).start()

    lax.fori_loop(0, chips, first, None)

    def couple_in(i, _):
        j = peer(lax.rem(i, chips))
        layer(0, j).wait_recv()
        layer(1, j).wait_recv()
        fields = []
        for n in range(2 * steps):
            _, pairs = sides(w, j, (n,))
            value = fg[j, n]
            base = 0 if n < steps else 6
            for d in range(3):
                value = value + cn[j, base + 2 * d] * pairs[d][0] + cn[j, base + 2 * d + 1] * pairs[d][1]
            fg[j, n] = value
            fields.append(value)
        b1, b2, mf, _ = waves(j)
        totals(1, j, fields[:steps], fields[steps:], b1, b2, mf)

    lax.fori_loop(1, chips + 1, couple_in, None)
    gather(1)
    scan(1)

    def stores(j):
        lanes = pl.ds(pl.multiple_of(j * LANES, LANES), LANES)
        return [
            pltpu.make_async_copy(out.at[j, pl.ds(0, steps)], s_hbm.at[:, :, lanes], osem.at[0, j]),
            pltpu.make_async_copy(out.at[j, pl.ds(steps, steps)], p_hbm.at[:, :, lanes], osem.at[1, j]),
        ]

    def last(i, _):
        j = peer(i)

        def store(n, value):
            out[j, n] = value

        solve(1, j, store)
        for copy in stores(j):
            copy.start()

    lax.fori_loop(0, chips, last, None)

    def drain(j, _):
        for copy in stores(j):
            copy.wait()
        for k in range(2):
            to_other(k, j).wait_send()
            to_other_back(k, j).wait_send()
        for direction in range(2):
            layer(direction, j).wait_send()

    lax.fori_loop(0, chips, drain, None)

    def drain_peers(i, _):
        for k in range(2):
            to_owner(k, peer(i)).wait_send()
            back(k, peer(i)).wait_send()

    lax.fori_loop(1, chips, drain_peers, None)


def solution(mesh):
    chips = mesh.shape["tm"] // 2
    slabs = mesh.shape["gz"]
    row = 4 if chips % 4 == 0 and chips > 4 else 2

    def body(state_rhs, adjoint_rhs, diffusivity, velocity):
        steps = state_rhs.shape[0]
        chunk = (ROWS, LANES)
        f32 = jnp.float32
        wide = (ROWS + 2 * PAD, LANES)
        hbm = pl.BlockSpec(memory_space=pl.ANY)
        dma = pltpu.SemaphoreType.DMA
        return pl.pallas_call(
            functools.partial(kernel, chips, row, slabs),
            out_shape=[jax.ShapeDtypeStruct(state_rhs.shape, f32)] * 2,
            in_specs=[hbm] * 4,
            out_specs=[hbm] * 2,
            scratch_shapes=[
                pltpu.VMEM((chips, 2 * steps) + chunk, f32),
                pltpu.VMEM((chips,) + wide, f32),
                pltpu.VMEM((chips, 3) + chunk, f32),
                pltpu.VMEM((chips, 4) + chunk, f32),
                pltpu.VMEM((chips, 12) + chunk, f32),
                pltpu.VMEM((chips, 2 * steps) + wide, f32),
                pltpu.VMEM((chips, 2 * steps) + chunk, f32),
                pltpu.VMEM((2, 2, chips) + chunk, f32),
                pltpu.VMEM((2, chips) + chunk, f32),
                pltpu.VMEM((2, chips) + chunk, f32),
                pltpu.VMEM((2, chips) + chunk, f32),
                pltpu.VMEM((2, chips) + chunk, f32),
                pltpu.VMEM((2, 2, chips) + chunk, f32),
                pltpu.VMEM((2, chips) + chunk, f32),
                dma((4, chips)),
                dma((2, chips)),
                dma((2,)),
                dma((2,)),
                dma((2, chips)),
                dma((2, chips)),
                dma((2, 4, chips)),
                dma((2, 4, chips)),
            ],
            compiler_params=pltpu.CompilerParams(
                collective_id=0, has_side_effects=True, vmem_limit_bytes=32 * 1024 * 1024),
        )(state_rhs, adjoint_rhs, diffusivity, velocity)

    placed = (P("tm", "gz", None), P("tm", "gz", None), P("gz", None), P(None, "gz", None))
    return jax.shard_map(
        body,
        mesh=mesh,
        in_specs=placed,
        out_specs=(P("tm", "gz", None), P("tm", "gz", None)),
        check_vma=False,
    )
```

time: 901 us -> 57.5 us (0.06); the launches traced: 891 us -> 57.2 us
  waiting for transfers between devices: 680 us -> 0 us
  other arithmetic: 98.3 us -> 0 us
  Pallas kernels: 0 us -> 50.1 us
  local copies, waits for them, and re-layouts: 42 us -> 6.47 us
  matrix products: 35.5 us -> 0 us
  starting transfers between devices: 33 us -> 0 us
    ppermute x14 -> x0, waiting for transfers between devices: 680 us -> none  [the longest x10 679 us: swapped(): return lax.ppermute(value, axis, pairs)]
    pallas_call x0 -> x1, Pallas kernels: none -> 50.1 us  [body(): pl.pallas_call(functools.partial(kernel, chips, row, slabs), out_shape=[j...]
    select_n x14 -> x0, other arithmetic: 40.1 us -> none  [the longest x4 23.9 us: body(): data = jnp.where(high, turned, data + partner)]
    dot_general x8 -> x0, matrix products: 35.5 us -> none  [mix_rows(): jnp.einsum('ab,sbm->sam', matrix, data, precision=lax.Precision.HIGHEST)]
    ppermute x14 -> x0, starting transfers between devices: 33 us -> none  [the longest x10 23.3 us: swapped(): return lax.ppermute(value, axis, pairs)]
    slice x12 -> x0, local copies, waits for them, and re-layouts: 25.2 us -> none  [the longest x2 9.67 us: ahead_flat(): field[..., stride:]]
    sub x9 -> x0, other arithmetic: 19.4 us -> none  [the longest x4 16.3 us: body(): spread = partner - data]
    add x7 -> x0, other arithmetic: 16.2 us -> none  [the longest x1 12.3 us: body(): blocks + coupling(first, first_pad, weights, velocity, NY)]
  transfers between devices with their start and end apart: 14 -> 0, of which waited for: 10 -> 0; matrix products, arithmetic and copies ran while one was open for 2% -> 0% of each run, Pallas kernels for 0% -> 0%
where the time goes in v1:
time: 57.5 us; the launch traced here: 57.2 us
  Pallas kernels  50.1 us (87%)
  local copies, waits for them, and re-layouts  6.47 us (11%)
  between operations  0.65 us (1%)
    pallas_call x1, Pallas kernels, body(): pl.pallas_call(functools.partial(kernel, chips, row, slabs), out_shape=[j...  50.1 us
    unnamed x10, local copies, waits for them, and re-layouts  6.47 us

profile of v1, /device:TPU:1, one launch (start us, length us, event | category | flops | bytes accessed | tf_op | source)
XLA Modules:
  0.0 57.2 jit_solution(12859497231727329969)
XLA Ops:
  0.6 0.0 copy-start
  0.6 1.2 %copy-done = f32[4,32,2048]{2,1,0:T(8,128)S(1)} copy-done((f32[4,32,2048]{2,1,0:T(8,128)S(1)}, f32[4,32,2048]{2,1,0:T(8,128)}, u32[]{:S(2)}) %copy-start) | copy-done | bytes 1048600
  1.9 0.0 copy-start.1
  1.9 1.2 %copy-done.1 = f32[4,32,2048]{2,1,0:T(8,128)S(1)} copy-done((f32[4,32,2048]{2,1,0:T(8,128)S(1)}, f32[4,32,2048]{2,1,0:T(8,128)}, u32[]{:S(2)}) %copy-start.1) | copy-done | bytes 1048600
  3.1 0.0 copy-start.2
  3.1 1.1 %copy-done.2 = f32[3,32,2048]{2,1,0:T(8,128)S(1)} copy-done((f32[3,32,2048]{2,1,0:T(8,128)S(1)}, f32[3,32,2048]{2,1,0:T(8,128)}, u32[]{:S(2)}) %copy-start.2) | copy-done | bytes 786456
  4.2 0.0 copy-start.3
  4.2 0.9 %copy-done.3 = f32[32,2048]{1,0:T(8,128)S(1)} copy-done((f32[32,2048]{1,0:T(8,128)S(1)}, f32[32,2048]{1,0:T(8,128)}, u32[]{:S(2)}) %copy-start.3) | copy-done | bytes 262168
  5.2 50.1 %shard_map.59 = (f32[4,32,2048]{2,1,0:T(8,128)S(1)}, f32[4,32,2048]{2,1,0:T(8,128)S(1)}) custom-call(f32[4,32,2048]{2,1,0:T(8,128)S(1)} %copy-done, f32[4,32,2048]{2,1,0:T(8,128)S(1)} %copy-done.1, f32[32,2048]{1,0:T(8,128)S(1)} %copy-done.3, f32[3,32,2048]{2,1,0:T(8,128)S(1)} %copy-done.2), custom_call_target="tpu_custom_call" | custom-call | tf_op jit(solution)/shard_map/pallas_call | solution.py:379
  55.3 1.0 %copy.8 = f32[4,32,2048]{2,1,0:T(8,128)} copy(f32[4,32,2048]{2,1,0:T(8,128)S(1)} %get-tuple-element.4) | data formatting | bytes 2097152
  56.2 1.0 %copy.9 = f32[4,32,2048]{2,1,0:T(8,128)} copy(f32[4,32,2048]{2,1,0:T(8,128)S(1)} %get-tuple-element.5) | data formatting | bytes 2097152
Async XLA Ops:
  0.6 1.2 %copy-start = (f32[4,32,2048]{2,1,0:T(8,128)S(1)}, f32[4,32,2048]{2,1,0:T(8,128)}, u32[]{:S(2)}) copy-start(f32[4,32,2048]{2,1,0:T(8,128)} %f_hbm.1) | copy-start | bytes 3145732
  1.9 1.2 %copy-start.1 = (f32[4,32,2048]{2,1,0:T(8,128)S(1)}, f32[4,32,2048]{2,1,0:T(8,128)}, u32[]{:S(2)}) copy-start(f32[4,32,2048]{2,1,0:T(8,128)} %g_hbm.1) | copy-start | bytes 3145732
  3.1 1.1 %copy-start.2 = (f32[3,32,2048]{2,1,0:T(8,128)S(1)}, f32[3,32,2048]{2,1,0:T(8,128)}, u32[]{:S(2)}) copy-start(f32[3,32,2048]{2,1,0:T(8,128)} %v_hbm.1) | copy-start | bytes 2359300
  4.2 0.9 %copy-start.3 = (f32[32,2048]{1,0:T(8,128)S(1)}, f32[32,2048]{1,0:T(8,128)}, u32[]{:S(2)}) copy-start(f32[32,2048]{1,0:T(8,128)} %k_hbm.1) | copy-start | bytes 786436
